TPU v7x, 32 devices: a whole 2x2x4 slice. The times are simulated.
32 devices in a mesh: dp: 4 (over y, x), fsdp: 8 (over z, core).
Axes of the slice: x: 2, y: 2, z: 4, core: 2. Of those that a mesh axis runs over, the one named last changes fastest.
Arguments:
- hidden: bfloat16 [2, 4608, 4096], P(None, ('dp', 'fsdp')), may hold values from -120 to 120
- cotangent: bfloat16 [2, 4608, 1024], P(None, ('dp', 'fsdp')), may hold values from -6 to 6
- proj_weight: bfloat16 [2, 4096, 1024], P(None, 'fsdp'), may hold values from -3 to 3
- norm_gain: float32 [2, 4096], replicated, may hold values from 0.1 to 1.9
- prev_factor: bfloat16 [2, 512, 128], replicated, may hold values from -0.25 to 0.25
- factor_ranks: int32 [2, 2], replicated, may hold values from 4 to 64, as said below
- layer_order: int32 [2], replicated, may hold values from 0 to 1, each once
Outputs:
- hidden_grad: bfloat16 [4608, 4096], P(('dp', 'fsdp'))
- basis_factor: float32 [2, 4096, 128], P(None, 'fsdp')
Inputs may be any that keep to these rules, and one draw needn't show every extreme that they name: `factor_ranks`: every draw holds a rank equal to 64 and a rank equal to 4.
All inputs are finite; a program needn't handle non-finite values.
Results may differ from a plain program's by a relative error of at most 0.0056.
Values may be sent and summed in bfloat16 or wider, within the bound.
A program may use at most 64 MiB of HBM per device.

v0:
```python
import math
import jax
import jax.numpy as jnp
from jax import lax
from jax.sharding import PartitionSpec as P

D = 4096


def normalize(hidden_rows, gain_row):
    wide_rows = hidden_rows.astype(jnp.float32)
    inverse = lax.rsqrt(jnp.mean(wide_rows * wide_rows, axis=1, keepdims=True) + 1e-05)
    normed = (wide_rows * inverse * gain_row[None, :]).astype(jnp.bfloat16)
    return (inverse, normed)


def masked_factors(factors, rank_pair):
    rank_cols = factors.shape[1] // 2
    position = jnp.arange(2 * rank_cols)
    column = position % rank_cols
    column_limit = jnp.where(position < rank_cols, rank_pair[0], rank_pair[1])
    return jnp.where((column < column_limit)[None, :], factors, jnp.zeros_like(factors))


def project(grad_rows, kept_factor):
    head_cols = grad_rows.shape[1] // 2
    rank_cols = kept_factor.shape[1] // 2
    keys_part = jnp.dot(
        grad_rows[:, :head_cols], kept_factor[:, :rank_cols], preferred_element_type=jnp.float32
    )
    values_part = jnp.dot(
        grad_rows[:, head_cols:], kept_factor[:, rank_cols:], preferred_element_type=jnp.float32
    )
    return jnp.concatenate([keys_part, values_part], axis=1).astype(jnp.bfloat16)


def gram_pair(factor_shard):
    row_count = factor_shard.shape[0]
    rank_cols = factor_shard.shape[1] // 2
    paired = factor_shard.reshape(row_count, 2, rank_cols)
    return jnp.einsum(
        "rmi,rmj->mij",
        paired,
        paired,
        precision=lax.Precision.HIGHEST,
        preferred_element_type=jnp.float32,
    )


def orthonormal(factor_shard, gram_totals, rank_pair):
    rank_cols = factor_shard.shape[1] // 2
    column = jnp.arange(rank_cols)
    pieces = []
    for member in range(2):
        block_cols = factor_shard[:, member * rank_cols : (member + 1) * rank_cols]
        padded = gram_totals[member] + jnp.diag((column >= rank_pair[member]).astype(jnp.float32))
        lower_factor = jnp.linalg.cholesky(padded)
        pieces.append(
            lax.linalg.triangular_solve(
                lower_factor, block_cols, left_side=False, lower=True, transpose_a=True
            )
        )
    return math.sqrt(D) * jnp.concatenate(pieces, axis=1)


def body(hidden, cotangent, proj_weight, norm_gain, prev_factor, factor_ranks, layer_order):
    layer_count = hidden.shape[0]
    top_slot = layer_order[0]
    inverses = []
    shards = []
    basis_list = []
    for slot_index in range(layer_count):
        inverse, normed = normalize(hidden[slot_index], norm_gain[slot_index])
        inverses.append(inverse)
        kept_factor = masked_factors(prev_factor[slot_index], factor_ranks[slot_index])
        projected = project(cotangent[slot_index], kept_factor)
        local_rows = lax.psum_scatter(
            lax.dot_general(
                normed, projected, (((0,), (0,)), ((), ())), preferred_element_type=jnp.float32
            ),
            "fsdp",
            scatter_dimension=0,
            tiled=True,
        )
        factor_shard = lax.psum(local_rows, "dp")
        shards.append(factor_shard)
    stacked = jnp.stack([gram_pair(factor_shard) for factor_shard in shards])
    all_grams = lax.psum(stacked, "fsdp")
    basis_list = [
        orthonormal(shards[slot_index], all_grams[slot_index], factor_ranks[slot_index])
        for slot_index in range(layer_count)
    ]
    top_grads = lax.dynamic_index_in_dim(cotangent, top_slot, 0, keepdims=False)
    top_weight = lax.dynamic_index_in_dim(proj_weight, top_slot, 0, keepdims=False)
    input_grad = lax.dot_general(
        top_grads,
        lax.all_gather(top_weight, "fsdp", axis=0, tiled=True),
        (((1,), (1,)), ((), ())),
        preferred_element_type=jnp.float32,
    )
    top_inverse = lax.dynamic_index_in_dim(jnp.stack(inverses), top_slot, 0, keepdims=False)
    top_gain = lax.dynamic_index_in_dim(norm_gain, top_slot, 0, keepdims=False)
    top_hidden = lax.dynamic_index_in_dim(hidden, top_slot, 0, keepdims=False).astype(jnp.float32)
    scaled = input_grad * top_gain[None, :]
    unit_rows = top_hidden * top_inverse
    inner_mean = jnp.mean(scaled * unit_rows, axis=1, keepdims=True)
    hidden_grad = (top_inverse * (scaled - unit_rows * inner_mean)).astype(jnp.bfloat16)
    return (hidden_grad, jnp.stack(basis_list))


def solution(mesh):
    in_specs = (
        P(None, ("dp", "fsdp"), None),
        P(None, ("dp", "fsdp"), None),
        P(None, "fsdp", None),
        P(),
        P(),
        P(),
        P(),
    )
    out_specs = (P(("dp", "fsdp"), None), P(None, "fsdp", None))
    return jax.shard_map(body, mesh=mesh, in_specs=in_specs, out_specs=out_specs, check_vma=False)
```

profile of v0, /device:TPU:0, one launch (start us, length us, event | category | flops | bytes accessed | tf_op | source)
XLA Modules:
  0.0 299.6 jit_solution(16446004569142756650)
XLA Ops:
  7.2 1.2 slice_bitcast_fusion.1
  8.5 1.4 fusion.76
  9.9 2.4 fusion.71
  12.3 1.0 bitcast_select_fusion.1
  13.9 2.2 fusion.8
  16.2 3.5 %fusion.17 = f32[4096,128]{1,0:T(8,128)} fusion(f32[4096]{0:T(1024)S(1)} %bitcast.139, f32[144]{0:T(256)S(1)} %add_rsqrt_fusion, bf16[2,144,4096]{2,1,0:T(8,128)(2,1)} %param.10, bf16[144,64]{0,1:T(8,128)(2,1)S(1)} %fusion.30, bf16[144,64]{0,1:T(8,128)(2,1)S(1)} %fusion.29), kind=kOutput, calls=%fused_computation.20 | convolution fusion | flops 153427968 | bytes 3330624 | tf_op jit(solution)/shard_map/dot_general | solution.py:78
  20.3 3.5 %fusion.19 = f32[4096,128]{1,0:T(8,128)} fusion(f32[4096]{0:T(1024)S(1)} %bitcast.138, f32[144]{0:T(256)S(1)} %add_rsqrt_fusion.1, bf16[2,144,4096]{2,1,0:T(8,128)(2,1)} %param.10, bf16[144,64]{0,1:T(8,128)(2,1)S(1)} %fusion.28, bf16[144,64]{0,1:T(8,128)(2,1)S(1)} %fusion.27), kind=kOutput, calls=%fused_computation.21 | convolution fusion | flops 153427968 | bytes 3330624 | tf_op jit(solution)/shard_map/dot_general | solution.py:78
  23.8 34.8 %reduce-scatter.5.cloned.1.call-done = f32[512,128]{1,0:T(8,128)} async-done(((f32[4096,128]{1,0:T(8,128)}), f32[512,128]{1,0:T(8,128)}) %reduce-scatter.5.cloned.1.call-update) | async-done | bytes 262160 | tf_op jit(solution)/shard_map/reduce_scatter | solution.py:77
  58.6 37.0 %reduce-scatter.3.cloned.1.call-done = f32[512,128]{1,0:T(8,128)} async-done(((f32[4096,128]{1,0:T(8,128)}), f32[512,128]{1,0:T(8,128)}) %reduce-scatter.3.cloned.1.call-update) | async-done | bytes 262160 | tf_op jit(solution)/shard_map/reduce_scatter | solution.py:77
  95.6 47.0 %all-reduce.6.cloned.1.call-done = (f32[512,128]{1,0:T(8,128)}, f32[512,128]{1,0:T(8,128)}) async-done(((f32[512,128]{1,0:T(8,128)}, f32[512,128]{1,0:T(8,128)}), (f32[512,128]{1,0:T(8,128)}, f32[512,128]{1,0:T(8,128)})) %all-reduce.6.cloned.1.call-update) | async-done | bytes 524304 | tf_op jit(solution)/shard_map/psum | solution.py:85
  142.7 1.1 copy.22
  144.1 1.1 copy.20
  145.6 0.7 pad_maximum_fusion.1
  146.6 1.0 constant_dynamic-slice_fusion.1
  147.6 1.3 compare_convert_fusion.2
  148.9 1.2 compare_convert_fusion
  150.1 51.2 %all-reduce.4.cloned.1.call-done = f32[2,2,64,64]{2,3,1,0:T(8,128)} async-done(((f32[2,2,64,64]{2,3,1,0:T(8,128)}), f32[2,2,64,64]{2,3,1,0:T(8,128)}) %all-reduce.4.cloned.1.call-update) | async-done | bytes 65552 | tf_op jit(solution)/shard_map/psum | solution.py:88
  201.4 0.8 fusion.60
  202.3 5.8 %cholesky.107 = f32[64,64]{1,0:T(8,128)S(1)} custom-call(f32[64,64]{1,0:T(8,128)S(1)} %fusion.62), custom_call_target="Cholesky" | custom-call | tf_op jit(solution)/shard_map/jit(cholesky)/cholesky | solution.py:57
  208.8 0.7 fusion.56
  209.5 4.9 %custom-call.11 = f32[1,64,64]{1,2,0:T(8,128)S(1)} custom-call(f32[1,64,64]{2,1,0:T(8,128)S(1)} %fusion.56), custom_call_target="InvertDiagBlocksLowerTriangular" | custom-call | tf_op jit(solution)/shard_map/triangular_solve/custom-call.0 | solution.py:59
  214.5 5.8 %cholesky.96 = f32[64,64]{1,0:T(8,128)S(1)} custom-call(f32[64,64]{1,0:T(8,128)S(1)} %fusion.64), custom_call_target="Cholesky" | custom-call | tf_op jit(solution)/shard_map/jit(cholesky)/cholesky | solution.py:57
  221.7 4.9 %custom-call.10 = f32[1,64,64]{1,2,0:T(8,128)S(1)} custom-call(f32[1,64,64]{2,1,0:T(8,128)S(1)} %fusion.55), custom_call_target="InvertDiagBlocksLowerTriangular" | custom-call | tf_op jit(solution)/shard_map/triangular_solve/custom-call.0 | solution.py:59
  226.7 5.8 %cholesky.85 = f32[64,64]{1,0:T(8,128)S(1)} custom-call(f32[64,64]{1,0:T(8,128)S(1)} %fusion.66), custom_call_target="Cholesky" | custom-call | tf_op jit(solution)/shard_map/jit(cholesky)/cholesky | solution.py:57
  233.9 4.9 %custom-call.9 = f32[1,64,64]{1,2,0:T(8,128)S(1)} custom-call(f32[1,64,64]{2,1,0:T(8,128)S(1)} %fusion.54), custom_call_target="InvertDiagBlocksLowerTriangular" | custom-call | tf_op jit(solution)/shard_map/triangular_solve/custom-call.0 | solution.py:59
  238.9 5.8 %cholesky.74 = f32[64,64]{1,0:T(8,128)S(1)} custom-call(f32[64,64]{1,0:T(8,128)S(1)} %fusion.68), custom_call_target="Cholesky" | custom-call | tf_op jit(solution)/shard_map/jit(cholesky)/cholesky | solution.py:57
  245.4 0.7 fusion.53
  246.1 4.9 %custom-call.8 = f32[1,64,64]{1,2,0:T(8,128)S(1)} custom-call(f32[1,64,64]{2,1,0:T(8,128)S(1)} %fusion.53), custom_call_target="InvertDiagBlocksLowerTriangular" | custom-call | tf_op jit(solution)/shard_map/triangular_solve/custom-call.0 | solution.py:59
  253.0 1.0 copy.28
  254.0 30.6 %all-gather.3.cloned.1.call-done = bf16[1,4096,1024]{2,1,0:T(8,128)(2,1)} async-done(((bf16[1,512,1024]{2,1,0:T(8,128)(2,1)}), bf16[1,4096,1024]{2,1,0:T(8,128)(2,1)}) %all-gather.3.cloned.1.call-update) | async-done | bytes 8388624 | tf_op jit(solution)/shard_map/all_gather | solution.py:97
  284.6 6.9 %fusion.13 = (f32[144]{0:T(256)S(1)}, f32[144,4096]{1,0:T(8,128)S(1)}) fusion(f32[144]{0:T(256)S(1)} %bitcast.141, bf16[2,144,4096]{2,1,0:T(8,128)(2,1)} %param.10, s32[]{:T(128)S(6)} %select_n.69, f32[4096]{0:T(1024)S(1)} %bitcast.140, bf16[1,4096,1024]{2,1,0:T(8,128)(2,1)} %all-gather.3.cloned.1.call-done, bf16[2,144,1024]{2,1,0:T(8,128)(2,1)S(1)} %copy-done.4), kind=kOutput, calls=%fused_computation.16 | convolution fusion | flops 1210908544 | bytes 12241472 | tf_op jit(solution)/shard_map/dot_general | solution.py:95
  291.5 1.6 fusion.16
  (60 shorter events, 8.8 us)
Async XLA Ops:
  7.2 139.4 %copy-start = (bf16[2,512,1024]{2,1,0:T(8,128)(2,1)S(1)}, bf16[2,512,1024]{2,1,0:T(8,128)(2,1)}, u32[]{:S(2)}) copy-start(bf16[2,512,1024]{2,1,0:T(8,128)(2,1)} %param.12) | copy-start | bytes 6291460
  7.2 6.7 %copy-start.6 = (s32[2]{0:T(128)S(1)}, s32[2]{0:T(128)}, u32[]{:S(2)}) copy-start(s32[2]{0:T(128)} %param.16) | copy-start | bytes 28
  7.2 9.0 %copy-start.5 = (f32[2,4096]{1,0:T(2,128)S(1)}, f32[2,4096]{1,0:T(2,128)}, u32[]{:S(2)}) copy-start(f32[2,4096]{1,0:T(2,128)} %param.13) | copy-start | bytes 98308
  7.2 51.4 %reduce-scatter.5.cloned.1.call-start = ((), (), s32[]{:S(2)}) async-start(), calls=%async_computation.3 | async-start | bytes 2359296 | tf_op jit(solution)/shard_map/reduce_scatter | solution.py:77
  19.7 75.8 %reduce-scatter.3.cloned.1.call-start = ((), (), s32[]{:S(2)}) async-start(), calls=%async_computation.2 | async-start | bytes 2359296 | tf_op jit(solution)/shard_map/reduce_scatter | solution.py:77
  23.8 118.9 %all-reduce.6.cloned.1.call-start = ((), (), s32[]{:S(2)}) async-start(), calls=%async_computation.6 | async-start | bytes 1048576 | tf_op jit(solution)/shard_map/psum | solution.py:85
  95.6 105.8 %all-reduce.4.cloned.1.call-start = ((), (), s32[]{:S(2)}) async-start(), calls=%async_computation.4 | async-start | bytes 262144 | tf_op jit(solution)/shard_map/psum | solution.py:88
  146.3 104.7 %copy-start.3 = (f32[512,128]{1,0:T(8,128)S(1)}, f32[512,128]{1,0:T(8,128)}, u32[]{:S(2)}) copy-start(f32[512,128]{1,0:T(8,128)} %get-tuple-element.10) | copy-start | bytes 786436
  146.3 138.2 %all-gather.3.cloned.1.call-start = ((), (), s32[]{:S(2)}) async-start(), calls=%async_computation.5 | async-start | bytes 9437184 | tf_op jit(solution)/shard_map/all_gather | solution.py:97
  147.6 104.4 %copy-start.2 = (f32[512,128]{1,0:T(8,128)S(1)}, f32[512,128]{1,0:T(8,128)}, u32[]{:S(2)}) copy-start(f32[512,128]{1,0:T(8,128)} %get-tuple-element.11) | copy-start | bytes 786436
  251.0 33.6 %copy-start.4 = (bf16[2,144,1024]{2,1,0:T(8,128)(2,1)S(1)}, bf16[2,144,1024]{2,1,0:T(8,128)(2,1)}, u32[]{:S(2)}) copy-start(bf16[2,144,1024]{2,1,0:T(8,128)(2,1)} %param.11) | copy-start | bytes 1769476
  284.6 6.9 %copy-start.1 = (bf16[2,144,4096]{2,1,0:T(8,128)(2,1)S(1)}, bf16[2,144,4096]{2,1,0:T(8,128)(2,1)}, u32[]{:S(2)}) copy-start(bf16[2,144,4096]{2,1,0:T(8,128)(2,1)} %param.10) | copy-start | bytes 7077892
Sparse Core Ops, SparseCore 0:
  19.9 38.7 reduce-scatter.4
  60.9 34.6 reduce-scatter.2
  98.6 44.0 all-reduce.5
  146.4 54.8 all-reduce.3
  203.4 81.1 all-gather.2
where the time goes:
time: 300 us
  waiting for transfers between devices  201 us (67%)
  other arithmetic  59.6 us (20%)
  matrix products  17.6 us (6%)
  between operations  14.2 us (5%)
  local copies, waits for them, and re-layouts  7.26 us (2%)
    reduce_scatter x2, waiting for transfers between devices, body(): lax.psum_scatter(lax.dot_general(normed, projected, (((0,), (0,)), ((), (...  71.7 us
    psum x1, waiting for transfers between devices, body(): all_grams = lax.psum(stacked, 'fsdp')  51.2 us
    psum x1, waiting for transfers between devices, body(): factor_shard = lax.psum(local_rows, 'dp')  47 us
    all_gather x1, waiting for transfers between devices, body(): lax.all_gather(top_weight, 'fsdp', axis=0, tiled=True)  30.6 us
    another operation x12, other arithmetic, orthonormal(): lower_factor = jnp.linalg.cholesky(padded)  26.1 us
    another operation x8, other arithmetic, orthonormal(): lax.linalg.triangular_solve(lower_factor, block_cols, left_side=False, lo...  22.2 us
    dot_general x2, matrix products, body(): lax.dot_general(normed, projected, (((0,), (0,)), ((), ())), preferred_el...  6.96 us
    dot_general x1, matrix products, body(): lax.dot_general(top_grads, lax.all_gather(top_weight, 'fsdp', axis=0, til...  6.9 us
  transfers between devices with their start and end apart: 5, of which 5 were waited for; matrix products, arithmetic and copies ran while one was open for 20% of the time, Pallas kernels for 0%

commit v1 on v0

--- a/solution.py
+++ b/solution.py
@@ -85,7 +85,7 @@
         factor_shard = lax.psum(local_rows, "dp")
         shards.append(factor_shard)
     stacked = jnp.stack([gram_pair(factor_shard) for factor_shard in shards])
-    all_grams = lax.psum(stacked, "fsdp")
+    all_grams = jnp.sum(lax.all_gather(stacked, "fsdp"), axis=0)
     basis_list = [
         orthonormal(shards[slot_index], all_grams[slot_index], factor_ranks[slot_index])
         for slot_index in range(layer_count)

time: 300 us -> 245 us (0.82)
  waiting for transfers between devices: 201 us -> 117 us
  blocking collectives: 0 us -> 20.5 us
  other arithmetic: 59.6 us -> 66.8 us
    psum x1 -> x0, waiting for transfers between devices: 51.2 us -> none  [body(): all_grams = lax.psum(stacked, 'fsdp')]
    all_gather x1, waiting for transfers between devices: 30.6 us -> 4.72 us  [body(): lax.all_gather(top_weight, 'fsdp', axis=0, tiled=True)]
    all_gather x0 -> x1, blocking collectives: none -> 20.5 us  [body(): all_grams = jnp.sum(lax.all_gather(stacked, 'fsdp'), axis=0)]
    psum x1, waiting for transfers between devices: 47 us -> 40.4 us  [body(): factor_shard = lax.psum(local_rows, 'dp')]
  transfers between devices with their start and end apart: 5 -> 4, of which waited for: 5 -> 4; matrix products, arithmetic and copies ran while one was open for 20% -> 29% of each run, Pallas kernels for 0% -> 0%
where the time goes in v1:
time: 245 us
  waiting for transfers between devices  117 us (48%)
  other arithmetic  66.8 us (27%)
  blocking collectives  20.5 us (8%)
  matrix products  18.5 us (8%)
  between operations  14.2 us (6%)
  local copies, waits for them, and re-layouts  7.64 us (3%)
    reduce_scatter x2, waiting for transfers between devices, body(): lax.psum_scatter(lax.dot_general(normed, projected, (((0,), (0,)), ((), (...  71.8 us
    psum x1, waiting for transfers between devices, body(): factor_shard = lax.psum(local_rows, 'dp')  40.4 us
    another operation x12, other arithmetic, orthonormal(): lower_factor = jnp.linalg.cholesky(padded)  26.1 us
    another operation x8, other arithmetic, orthonormal(): lax.linalg.triangular_solve(lower_factor, block_cols, left_side=False, lo...  22.2 us
    all_gather x1, blocking collectives, body(): all_grams = jnp.sum(lax.all_gather(stacked, 'fsdp'), axis=0)  20.5 us
    dot_general x2, matrix products, body(): lax.dot_general(normed, projected, (((0,), (0,)), ((), ())), preferred_el...  6.96 us
    dot_general x1, matrix products, body(): lax.dot_general(top_grads, lax.all_gather(top_weight, 'fsdp', axis=0, til...  6.9 us
  transfers between devices with their start and end apart: 4, of which 4 were waited for; matrix products, arithmetic and copies ran while one was open for 29% of the time, Pallas kernels for 0%

profile of v1, /device:TPU:0, one launch (start us, length us, event | category | flops | bytes accessed | tf_op | source)
XLA Modules:
  0.0 244.8 jit_solution(5310999981650866182)
XLA Ops:
  7.2 1.2 slice_bitcast_fusion.1
  8.5 1.5 fusion.73
  10.0 2.6 %fusion.67 = (pred[128]{0:T(512)(128)(4,1)S(1)}, pred[128]{0:T(512)(128)(4,1)S(1)}) fusion(s32[]{:T(128)} %bitcast.13, s32[]{:T(128)} %bitcast.12, s32[]{:T(128)} %bitcast.23, s32[]{:T(128)} %bitcast.22), kind=kLoop, calls=%fused_computation.122 | loop fusion | flops 1408 | bytes 272 | tf_op jit(solution)/shard_map/lt | solution.py:22
  12.6 1.0 bitcast_select_fusion.1
  14.1 2.2 fusion.8
  16.4 3.5 %fusion.17 = f32[4096,128]{1,0:T(8,128)} fusion(f32[4096]{0:T(1024)S(1)} %bitcast.141, f32[144]{0:T(256)S(1)} %add_rsqrt_fusion, bf16[2,144,4096]{2,1,0:T(8,128)(2,1)} %param.10, bf16[144,64]{0,1:T(8,128)(2,1)S(1)} %fusion.30, bf16[144,64]{0,1:T(8,128)(2,1)S(1)} %fusion.29), kind=kOutput, calls=%fused_computation.20 | convolution fusion | flops 153427968 | bytes 3330624 | tf_op jit(solution)/shard_map/dot_general | solution.py:78
  20.5 3.5 %fusion.19 = f32[4096,128]{1,0:T(8,128)} fusion(f32[4096]{0:T(1024)S(1)} %bitcast.140, f32[144]{0:T(256)S(1)} %add_rsqrt_fusion.1, bf16[2,144,4096]{2,1,0:T(8,128)(2,1)} %param.10, bf16[144,64]{0,1:T(8,128)(2,1)S(1)} %fusion.28, bf16[144,64]{0,1:T(8,128)(2,1)S(1)} %fusion.27), kind=kOutput, calls=%fused_computation.21 | convolution fusion | flops 153427968 | bytes 3330624 | tf_op jit(solution)/shard_map/dot_general | solution.py:78
  24.1 34.8 %reduce-scatter.5.cloned.1.call-done = f32[512,128]{1,0:T(8,128)} async-done(((f32[4096,128]{1,0:T(8,128)}), f32[512,128]{1,0:T(8,128)}) %reduce-scatter.5.cloned.1.call-update) | async-done | bytes 262160 | tf_op jit(solution)/shard_map/reduce_scatter | solution.py:77
  58.8 37.0 %reduce-scatter.3.cloned.1.call-done = f32[512,128]{1,0:T(8,128)} async-done(((f32[4096,128]{1,0:T(8,128)}), f32[512,128]{1,0:T(8,128)}) %reduce-scatter.3.cloned.1.call-update) | async-done | bytes 262160 | tf_op jit(solution)/shard_map/reduce_scatter | solution.py:77
  95.9 1.0 constant_dynamic-slice_fusion.1
  97.0 1.2 compare_convert_fusion
  98.2 1.3 compare_convert_fusion.1
  99.4 1.2 compare_convert_fusion.2
  100.7 1.2 compare_convert_fusion.3
  102.5 40.4 %all-reduce.3.cloned.1.call-done = (f32[512,128]{1,0:T(8,128)}, f32[512,128]{1,0:T(8,128)}) async-done(((f32[512,128]{1,0:T(8,128)}, f32[512,128]{1,0:T(8,128)}), (f32[512,128]{1,0:T(8,128)}, f32[512,128]{1,0:T(8,128)})) %all-reduce.3.cloned.1.call-update) | async-done | bytes 524304 | tf_op jit(solution)/shard_map/psum | solution.py:85
  142.9 1.1 copy.26
  144.0 1.1 copy.25
  145.8 20.5 %all-gather.1 = f32[16,2,64,64]{3,2,1,0:T(8,128)S(1)} all-gather(f32[2,2,64,64]{3,2,1,0:T(8,128)S(1)} %pad_maximum_fusion.1), channel_id=3, replica_groups=mesh['dp'=4,'fsdp'=8] {'fsdp'}, dimensions={0}, use_global_device_ids=true | all-gather | bytes 589824 | tf_op jit(solution)/shard_map/all_gather | solution.py:88
  166.5 0.7 bitcast_add_fusion.1
  168.0 5.8 %cholesky.107 = f32[64,64]{1,0:T(8,128)S(1)} custom-call(f32[64,64]{1,0:T(8,128)S(1)} %fusion.58), custom_call_target="Cholesky" | custom-call | tf_op jit(solution)/shard_map/jit(cholesky)/cholesky | solution.py:57
  175.2 4.9 %custom-call.11 = f32[1,64,64]{1,2,0:T(8,128)S(1)} custom-call(f32[1,64,64]{2,1,0:T(8,128)S(1)} %fusion.56), custom_call_target="InvertDiagBlocksLowerTriangular" | custom-call | tf_op jit(solution)/shard_map/triangular_solve/custom-call.0 | solution.py:59
  181.6 5.8 %cholesky.96 = f32[64,64]{1,0:T(8,128)S(1)} custom-call(f32[64,64]{1,0:T(8,128)S(1)} %fusion.60), custom_call_target="Cholesky" | custom-call | tf_op jit(solution)/shard_map/jit(cholesky)/cholesky | solution.py:57
  188.8 4.9 %custom-call.10 = f32[1,64,64]{1,2,0:T(8,128)S(1)} custom-call(f32[1,64,64]{2,1,0:T(8,128)S(1)} %fusion.55), custom_call_target="InvertDiagBlocksLowerTriangular" | custom-call | tf_op jit(solution)/shard_map/triangular_solve/custom-call.0 | solution.py:59
  195.2 5.8 %cholesky.85 = f32[64,64]{1,0:T(8,128)S(1)} custom-call(f32[64,64]{1,0:T(8,128)S(1)} %fusion.62), custom_call_target="Cholesky" | custom-call | tf_op jit(solution)/shard_map/jit(cholesky)/cholesky | solution.py:57
  202.4 4.9 %custom-call.9 = f32[1,64,64]{1,2,0:T(8,128)S(1)} custom-call(f32[1,64,64]{2,1,0:T(8,128)S(1)} %fusion.54), custom_call_target="InvertDiagBlocksLowerTriangular" | custom-call | tf_op jit(solution)/shard_map/triangular_solve/custom-call.0 | solution.py:59
  208.9 5.8 %cholesky.74 = f32[64,64]{1,0:T(8,128)S(1)} custom-call(f32[64,64]{1,0:T(8,128)S(1)} %fusion.64), custom_call_target="Cholesky" | custom-call | tf_op jit(solution)/shard_map/jit(cholesky)/cholesky | solution.py:57
  216.0 4.9 %custom-call.8 = f32[1,64,64]{1,2,0:T(8,128)S(1)} custom-call(f32[1,64,64]{2,1,0:T(8,128)S(1)} %fusion.53), custom_call_target="InvertDiagBlocksLowerTriangular" | custom-call | tf_op jit(solution)/shard_map/triangular_solve/custom-call.0 | solution.py:59
  221.0 1.5 convolution_bitcast_fusion
  224.0 1.0 copy.35
  225.0 4.7 %all-gather.4.cloned.1.call-done = bf16[1,4096,1024]{2,1,0:T(8,128)(2,1)} async-done(((bf16[1,512,1024]{2,1,0:T(8,128)(2,1)}), bf16[1,4096,1024]{2,1,0:T(8,128)(2,1)}) %all-gather.4.cloned.1.call-update) | async-done | bytes 8388624 | tf_op jit(solution)/shard_map/all_gather | solution.py:97
  229.7 6.9 %fusion.13 = (f32[144]{0:T(256)S(1)}, f32[144,4096]{1,0:T(8,128)S(1)}) fusion(f32[144]{0:T(256)S(1)} %bitcast.143, bf16[2,144,4096]{2,1,0:T(8,128)(2,1)} %param.10, s32[]{:T(128)S(6)} %select_n.69, f32[4096]{0:T(1024)S(1)} %bitcast.142, bf16[1,4096,1024]{2,1,0:T(8,128)(2,1)} %all-gather.4.cloned.1.call-done, bf16[2,144,1024]{2,1,0:T(8,128)(2,1)S(1)} %copy-done.4), kind=kOutput, calls=%fused_computation.16 | convolution fusion | flops 1210908544 | bytes 12241472 | tf_op jit(solution)/shard_map/dot_general | solution.py:95
  236.7 1.6 fusion.16
  (71 shorter events, 15.0 us)
Async XLA Ops:
  7.2 88.7 %copy-start = (bf16[2,512,1024]{2,1,0:T(8,128)(2,1)S(1)}, bf16[2,512,1024]{2,1,0:T(8,128)(2,1)}, u32[]{:S(2)}) copy-start(bf16[2,512,1024]{2,1,0:T(8,128)(2,1)} %param.12) | copy-start | bytes 6291460
  7.2 6.9 %copy-start.7 = (s32[2]{0:T(128)S(1)}, s32[2]{0:T(128)}, u32[]{:S(2)}) copy-start(s32[2]{0:T(128)} %param.16) | copy-start | bytes 28
  7.2 9.2 %copy-start.5 = (f32[2,4096]{1,0:T(2,128)S(1)}, f32[2,4096]{1,0:T(2,128)}, u32[]{:S(2)}) copy-start(f32[2,4096]{1,0:T(2,128)} %param.13) | copy-start | bytes 98308
  7.2 51.6 %reduce-scatter.5.cloned.1.call-start = ((), (), s32[]{:S(2)}) async-start(), calls=%async_computation.3 | async-start | bytes 2359296 | tf_op jit(solution)/shard_map/reduce_scatter | solution.py:77
  20.0 75.9 %reduce-scatter.3.cloned.1.call-start = ((), (), s32[]{:S(2)}) async-start(), calls=%async_computation.2 | async-start | bytes 2359296 | tf_op jit(solution)/shard_map/reduce_scatter | solution.py:77
  24.0 118.9 %all-reduce.3.cloned.1.call-start = ((), (), s32[]{:S(2)}) async-start(), calls=%async_computation.5 | async-start | bytes 1048576 | tf_op jit(solution)/shard_map/psum | solution.py:85
  95.8 133.9 %all-gather.4.cloned.1.call-start = ((), (), s32[]{:S(2)}) async-start(), calls=%async_computation.4 | async-start | bytes 9437184 | tf_op jit(solution)/shard_map/all_gather | solution.py:97
  166.3 56.7 %copy-start.2 = (f32[512,128]{1,0:T(8,128)S(1)}, f32[512,128]{1,0:T(8,128)}, u32[]{:S(2)}) copy-start(f32[512,128]{1,0:T(8,128)} %get-tuple-element.13) | copy-start | bytes 786436
  166.4 56.1 %copy-start.3 = (f32[512,128]{1,0:T(8,128)S(1)}, f32[512,128]{1,0:T(8,128)}, u32[]{:S(2)}) copy-start(f32[512,128]{1,0:T(8,128)} %get-tuple-element.12) | copy-start | bytes 786436
  220.9 8.8 %copy-start.4 = (bf16[2,144,1024]{2,1,0:T(8,128)(2,1)S(1)}, bf16[2,144,1024]{2,1,0:T(8,128)(2,1)}, u32[]{:S(2)}) copy-start(bf16[2,144,1024]{2,1,0:T(8,128)(2,1)} %param.11) | copy-start | bytes 1769476
  221.0 8.8 %copy-start.6 = (f32[1,144,1]{1,2,0:T(1,128)S(1)}, f32[1,144,1]{1,2,0:T(1,128)}, u32[]{:S(2)}) copy-start(f32[1,144,1]{1,2,0:T(1,128)} %fusion.66) | copy-start | bytes 1732
  229.7 6.9 %copy-start.1 = (bf16[2,144,4096]{2,1,0:T(8,128)(2,1)S(1)}, bf16[2,144,4096]{2,1,0:T(8,128)(2,1)}, u32[]{:S(2)}) copy-start(bf16[2,144,4096]{2,1,0:T(8,128)(2,1)} %param.10) | copy-start | bytes 7077892
Sparse Core Ops, SparseCore 0:
  20.1 38.7 reduce-scatter.4
  61.1 34.6 reduce-scatter.2
  98.8 44.0 all-reduce.2
  144.9 84.7 all-gather.3
